TPU v7x, 512 devices: a whole 4x4x16 slice. The times are simulated.
512 devices in a mesh: ctx: 64 (over y, z_lo, core), mp: 8 (over x, z_hi).
Axes of the slice: x: 4, y: 4, z: 16 (z_hi: 2, z_lo: 8; z = z_hi * 8 + z_lo), core: 2. Of those that a mesh axis runs over, the one named last changes fastest.
Arguments:
- stream: bfloat16 [4, 65536, 1024], P(None, 'ctx', 'mp'), may hold values from -40 to 40
- gain_mix: bfloat16 [1024], P('mp'), may hold values from 0.25 to 1.75
- proj_in: bfloat16 [8, 128, 384], P('mp'), may hold values from -0.5 to 0.5
- short_taps: float32 [3, 8, 384], P(None, 'mp'), may hold values from -3 to 3
- fwd_inner: bfloat16 [256, 256], replicated, may hold values from -0.375 to 0.375
- twid_inner: float32 [256, 256], P('ctx'), may hold values from -1.5 to 1.5
- fwd_outer: bfloat16 [256, 256], replicated, may hold values from -0.375 to 0.375
- kernel: bfloat16 [256, 256, 1024], P(None, 'ctx', 'mp'), may hold values from -4 to 4
- inv_outer: bfloat16 [256, 256], replicated, may hold values from -0.375 to 0.375
- backward_twiddle: float32 [256, 256], P(None, 'ctx'), may hold values from -1.5 to 1.5
- inv_inner: bfloat16 [256, 256], replicated, may hold values from -0.375 to 0.375
- proj_out: bfloat16 [8, 128, 128], P('mp'), may hold values from -0.5 to 0.5
- gain_mlp: bfloat16 [1024], P('mp'), may hold values from 0.25 to 1.75
- up_blocks: bfloat16 [8, 128, 512], P('mp'), may hold values from -0.5 to 0.5
- down_blocks: bfloat16 [8, 512, 128], P('mp'), may hold values from -0.25 to 0.25
Outputs:
- stream_out: bfloat16 [4, 65536, 1024], P(None, 'ctx', 'mp')
All inputs are finite; a program needn't handle non-finite values.
Results may differ from a plain program's by a relative error of at most 0.0085.
Values may be sent and summed in bfloat16 or wider, within the bound.
A program may use at most 64 MiB of HBM per device.

v0:
```python
import jax
import jax.numpy as jnp
from jax import lax
from jax.sharding import PartitionSpec as P

D = 1024
NB = 8


epsilon = 1e-05


def from_behind(array, axis, by):
    length = lax.axis_size(axis)
    pairs = [(i, i + by) for i in range(length) if 0 <= i + by < length]
    return lax.ppermute(array, axis, pairs)


def body(
    stream,
    gain_mix,
    proj_in,
    short_taps,
    fwd_inner,
    twid_inner,
    fwd_outer,
    kernel,
    inv_outer,
    backward_twiddle,
    inv_inner,
    proj_out,
    gain_mlp,
    up_blocks,
    down_blocks,
):
    seq_count, tok_count, width_here = stream.shape
    blocks_here, block_width = (proj_in.shape[0], proj_in.shape[1])
    root_len = fwd_inner.shape[0]
    rows_here = twid_inner.shape[0]
    sub_width = block_width // NB
    hid_block = up_blocks.shape[2]
    hid_sub = hid_block // NB
    x_float = stream.astype(jnp.float32)
    sumsq_mix = lax.psum(jnp.sum(x_float * x_float, axis=2), "mp")
    normed = (
        x_float * lax.rsqrt(sumsq_mix[..., None] / D + epsilon) * gain_mix.astype(jnp.float32)
    ).astype(jnp.bfloat16)
    u_blocks = normed.reshape(seq_count, tok_count, blocks_here, block_width)
    projected = jnp.einsum(
        "xtlc,lcd->xtld", u_blocks, proj_in, preferred_element_type=jnp.float32
    ).astype(jnp.bfloat16)
    rim_rows = projected[:, tok_count - 2 :]
    earlier = from_behind(rim_rows, "ctx", 1)
    padded = jnp.concatenate([earlier, projected], axis=1).astype(jnp.float32)
    mixed_all = (
        short_taps[0] * padded[:, 2:]
        + short_taps[1] * padded[:, 1 : tok_count + 1]
        + short_taps[2] * padded[:, :tok_count]
    )
    query_part = mixed_all[..., :block_width].astype(jnp.bfloat16)
    source = (
        mixed_all[..., block_width : 2 * block_width] * mixed_all[..., 2 * block_width :]
    ).astype(jnp.bfloat16)
    lattice = source.reshape(seq_count, rows_here, root_len, blocks_here, block_width)
    opening_segment = (
        jnp.einsum("xablc,bf->xaflc", lattice, fwd_inner, preferred_element_type=jnp.float32)
        * twid_inner[None, :, :, None, None]
    ).astype(jnp.bfloat16)
    kernel_blocks = kernel.reshape(root_len, kernel.shape[1], blocks_here, block_width)
    middle_segment = (
        jnp.einsum(
            "xaflc,ag->xgflc",
            lax.all_to_all(opening_segment, "ctx", split_axis=2, concat_axis=1, tiled=True),
            fwd_outer,
            preferred_element_type=jnp.float32,
        )
        * kernel_blocks[None]
    ).astype(jnp.bfloat16)
    closing_segment = (
        jnp.einsum("xgflc,gh->xhflc", middle_segment, inv_outer, preferred_element_type=jnp.float32)
        * backward_twiddle[None, :, :, None, None]
    ).astype(jnp.bfloat16)
    returned = lax.all_to_all(closing_segment, "ctx", split_axis=1, concat_axis=2, tiled=True)
    convolved = jnp.einsum(
        "xhflc,fe->lcxhe", returned, inv_inner, preferred_element_type=jnp.float32
    ).reshape(blocks_here, block_width, seq_count, tok_count)
    gated_out = (jnp.transpose(query_part, (2, 3, 0, 1)).astype(jnp.float32) * convolved).astype(
        jnp.bfloat16
    )
    spread = gated_out.reshape(blocks_here, NB, sub_width, seq_count, tok_count)
    out_table = proj_out.reshape(blocks_here, NB, sub_width, block_width)
    mix_out = jnp.einsum(
        "ijtxs,jitd->xsjd",
        lax.all_to_all(spread, "mp", split_axis=1, concat_axis=0, tiled=True),
        out_table,
        preferred_element_type=jnp.float32,
    )
    residual = (x_float.reshape(seq_count, tok_count, blocks_here, block_width) + mix_out).astype(
        jnp.bfloat16
    )
    resid_float = residual.astype(jnp.float32)
    sumsq_mlp = lax.psum(jnp.sum(resid_float * resid_float, axis=(2, 3)), "mp")
    gain_here = gain_mlp.astype(jnp.float32).reshape(blocks_here, block_width)
    normed_mlp = (
        resid_float * lax.rsqrt(sumsq_mlp[..., None, None] / D + epsilon) * gain_here
    ).astype(jnp.bfloat16)
    upper_part = jnp.einsum(
        "xslc,lch->lhxs", normed_mlp, up_blocks, preferred_element_type=jnp.float32
    )
    active = (
        jax.nn.gelu(upper_part)
        .astype(jnp.bfloat16)
        .reshape(blocks_here, NB, hid_sub, seq_count, tok_count)
    )
    down_table = down_blocks.reshape(blocks_here, NB, hid_sub, block_width)
    lower_part = jnp.einsum(
        "ijtxs,jitd->xsjd",
        lax.all_to_all(active, "mp", split_axis=1, concat_axis=0, tiled=True),
        down_table,
        preferred_element_type=jnp.float32,
    )
    output = (
        (resid_float + lower_part).astype(jnp.bfloat16).reshape(seq_count, tok_count, width_here)
    )
    return output


def solution(mesh):
    placed = (
        P(None, "ctx", "mp"),
        P("mp"),
        P("mp", None, None),
        P(None, "mp", None),
        P(),
        P("ctx", None),
        P(),
        P(None, "ctx", "mp"),
        P(),
        P(None, "ctx"),
        P(),
        P("mp", None, None),
        P("mp"),
        P("mp", None, None),
        P("mp", None, None),
    )
    return jax.shard_map(
        body, mesh=mesh, in_specs=placed, out_specs=P(None, "ctx", "mp"), check_vma=False
    )
```

profile of v0, /device:TPU:41, one launch (start us, length us, event | category | flops | bytes accessed | tf_op | source)
XLA Modules:
  0.0 548.8 jit_solution(4294799619383191293)
XLA Ops:
  0.0 1.5 copy.44
  1.8 73.5 %psum.14 = f32[4,1024]{1,0:T(4,128)S(1)} all-reduce(f32[4,1024]{1,0:T(4,128)S(1)} %fusion.15), channel_id=1, replica_groups=mesh['ctx'=64,'mp'=8] {'mp'}, use_global_device_ids=true, to_apply=%region_1.0 | all-reduce | flops 4096 | bytes 32768 | tf_op jit(solution)/shard_map/psum | solution.py:44
  75.3 0.7 convert_element_type.84
  75.9 2.0 convert_bitcast_fusion
  77.9 10.5 %collective-permute-start = (bf16[4,2,1,384]{3,1,0,2:T(2,128)(2,1)S(1)}, bf16[4,2,1,384]{3,1,0,2:T(2,128)(2,1)S(1)}, u32[]{:S(2)}, u32[]{:S(2)}) collective-permute-start(bf16[4,2,1,384]{3,1,0,2:T(2,128)(2,1)S(1)} %slice.41), channel_id=1, source_target_pairs={{0,8},{8,16},{16,24},{24,32},{32,40},{40,48},{48,56},{56,64},{64,7... | collective-permute-start | bytes 18440 | tf_op jit(solution)/shard_map/ppermute | solution.py:16
  88.5 0.7 collective-permute-done
  89.8 1.9 fusion.8
  91.7 2.7 copy-done.1
  94.6 0.7 copy-done.3
  95.8 1.8 copy.47
  97.6 14.6 %all-to-all-start = ((bf16[4,4,256,1,128]{4,1,0,3,2:T(4,128)(2,1)}), bf16[4,4,256,1,128]{4,1,0,3,2:T(4,128)(2,1)S(1)}, u32[]{:S(2)}, u32[]{:S(2)}) async-start(bf16[4,4,256,1,128]{4,1,0,3,2:T(4,128)(2,1)} %copy.47), calls=%async_computation | async-start | bytes 2097152 | tf_op jit(solution)/shard_map/all_to_all | solution.py:73
  112.2 1.0 copy.51
  113.2 49.1 %all-to-all-done = bf16[4,4,256,1,128]{4,1,0,3,2:T(4,128)(2,1)S(1)} async-done(((bf16[4,4,256,1,128]{4,1,0,3,2:T(4,128)(2,1)}), bf16[4,4,256,1,128]{4,1,0,3,2:T(4,128)(2,1)S(1)}, u32[]{:S(2)}, u32[]{:S(2)}) %all-to-all-start) | async-done | bytes 1048608 | tf_op jit(solution)/shard_map/all_to_all | solution.py:73
  162.6 0.8 copy.49
  163.5 1.9 fusion.30
  165.4 1.1 copy.52
  166.4 59.2 %all_to_all.48 = bf16[4,256,4,1,128]{4,2,0,3,1:T(4,128)(2,1)S(1)} all-to-all(bf16[4,256,4,1,128]{4,2,0,3,1:T(4,128)(2,1)S(1)} %copy.52), channel_id=1, replica_groups=mesh['ctx'=64,'mp'=8] {'ctx'}, dimensions={1} | all-to-all | bytes 2097152 | tf_op jit(solution)/shard_map/all_to_all | solution.py:83
  225.9 0.8 copy.54
  226.8 1.8 convolution_bitcast_fusion
  228.6 1.9 copy.56
  230.5 2.9 fusion.26
  233.4 1.5 copy.57
  234.9 1.0 copy.58
  236.0 3.6 all-to-all-start.2
  239.6 58.1 %all-to-all-done.2 = bf16[1,8,16,4,1024]{4,2,3,0,1:T(8,128)(2,1)S(1)} async-done(((bf16[1,8,16,4,1024]{4,2,3,0,1:T(8,128)(2,1)}), bf16[1,8,16,4,1024]{4,2,3,0,1:T(8,128)(2,1)S(1)}, u32[]{:S(2)}, u32[]{:S(2)}) %all-to-all-start.2) | async-done | bytes 1048608 | tf_op jit(solution)/shard_map/all_to_all | solution.py:94
  297.7 0.7 fusion.18
  298.4 59.3 %psum.15 = f32[4,1024]{1,0:T(4,128)S(1)} all-reduce(f32[4,1024]{1,0:T(4,128)S(1)} %get-tuple-element.8), channel_id=1, replica_groups=mesh['ctx'=64,'mp'=8] {'mp'}, use_global_device_ids=true, to_apply=%region_3.0 | all-reduce | flops 4096 | bytes 32768 | tf_op jit(solution)/shard_map/psum | solution.py:102
  357.7 3.3 fusion.7
  361.0 0.7 copy.62
  361.7 184.4 %all_to_all.49 = bf16[1,8,64,4,1024]{4,2,3,0,1:T(8,128)(2,1)S(1)} all-to-all(bf16[1,8,64,4,1024]{4,2,3,0,1:T(8,128)(2,1)S(1)} %copy.62), channel_id=1, replica_groups=mesh['ctx'=64,'mp'=8] {'mp'}, dimensions={1} | all-to-all | bytes 8388608 | tf_op jit(solution)/shard_map/all_to_all | solution.py:118
  546.1 1.4 fusion.31
  547.5 1.3 copy.65
  (35 shorter events, 2.2 us)
Async XLA Ops:
  0.0 357.7 %copy-start = (bf16[1,128,512]{2,1,0:T(8,128)(2,1)S(1)}, bf16[1,128,512]{2,1,0:T(8,128)(2,1)}, u32[]{:S(2)}) copy-start(bf16[1,128,512]{2,1,0:T(8,128)(2,1)} %param.28) | copy-start | bytes 393220
  0.0 88.4 %copy-start.7 = (f32[3,1,384]{2,1,0:T(1,128)S(1)}, f32[3,1,384]{2,1,0:T(1,128)}, u32[]{:S(2)}) copy-start(f32[3,1,384]{2,1,0:T(1,128)} %param.18) | copy-start | bytes 13828
  77.9 11.2 %collective-permute-start = (bf16[4,2,1,384]{3,1,0,2:T(2,128)(2,1)S(1)}, bf16[4,2,1,384]{3,1,0,2:T(2,128)(2,1)S(1)}, u32[]{:S(2)}, u32[]{:S(2)}) collective-permute-start(bf16[4,2,1,384]{3,1,0,2:T(2,128)(2,1)S(1)} %slice.41), channel_id=1, source_target_pairs={{0,8},{8,16},{16,24},{24,32},{32,40},{40,48},{48,56},{56,64},{64,7... | collective-permute-start | bytes 18440 | tf_op jit(solution)/shard_map/ppermute | solution.py:16
  91.7 2.7 copy-start.1
  94.4 0.9 copy-start.3
  94.4 0.9 copy-start.8
  94.6 17.6 %copy-start.2 = (bf16[256,4,128]{2,1,0:T(4,128)(2,1)S(1)}, bf16[256,4,128]{2,1,0:T(4,128)(2,1)}, u32[]{:S(2)}) copy-start(bf16[256,4,128]{2,1,0:T(4,128)(2,1)} %param.22) | copy-start | bytes 786436
  95.8 67.7 %copy-start.4 = (bf16[256,256]{1,0:T(8,128)(2,1)S(1)}, bf16[256,256]{1,0:T(8,128)(2,1)}, u32[]{:S(2)}) copy-start(bf16[256,256]{1,0:T(8,128)(2,1)} %param.23) | copy-start | bytes 393220
  95.8 67.7 %copy-start.5 = (bf16[256,256]{1,0:T(8,128)(2,1)S(1)}, bf16[256,256]{1,0:T(8,128)(2,1)}, u32[]{:S(2)}) copy-start(bf16[256,256]{1,0:T(8,128)(2,1)} %param.21) | copy-start | bytes 393220
  95.8 67.7 %copy-start.9 = (f32[256,4]{0,1:T(4,128)S(1)}, f32[256,4]{0,1:T(4,128)}, u32[]{:S(2)}) copy-start(f32[256,4]{0,1:T(4,128)} %param.24) | copy-start | bytes 12292
  97.6 64.8 %all-to-all-start = ((bf16[4,4,256,1,128]{4,1,0,3,2:T(4,128)(2,1)}), bf16[4,4,256,1,128]{4,1,0,3,2:T(4,128)(2,1)S(1)}, u32[]{:S(2)}, u32[]{:S(2)}) async-start(bf16[4,4,256,1,128]{4,1,0,3,2:T(4,128)(2,1)} %copy.47), calls=%async_computation | async-start | bytes 2097152 | tf_op jit(solution)/shard_map/all_to_all | solution.py:73
  165.3 61.4 %copy-start.6 = (bf16[256,256]{1,0:T(8,128)(2,1)S(1)}, bf16[256,256]{1,0:T(8,128)(2,1)}, u32[]{:S(2)}) copy-start(bf16[256,256]{1,0:T(8,128)(2,1)} %param.25) | copy-start | bytes 393220
  233.4 6.1 %copy-start.12 = (bf16[128]{0:T(256)(128)(2,1)S(1)}, bf16[128]{0:T(256)(128)(2,1)}, u32[]{:S(2)}) copy-start(bf16[128]{0:T(256)(128)(2,1)} %param.27) | copy-start | bytes 772
  233.4 64.3 %copy-start.11 = (bf16[1,128,128]{2,1,0:T(8,128)(2,1)S(1)}, bf16[1,128,128]{2,1,0:T(8,128)(2,1)}, u32[]{:S(2)}) copy-start(bf16[1,128,128]{2,1,0:T(8,128)(2,1)} %param.26) | copy-start | bytes 98308
  236.0 61.7 %all-to-all-start.2 = ((bf16[1,8,16,4,1024]{4,2,3,0,1:T(8,128)(2,1)}), bf16[1,8,16,4,1024]{4,2,3,0,1:T(8,128)(2,1)S(1)}, u32[]{:S(2)}, u32[]{:S(2)}) async-start(bf16[1,8,16,4,1024]{4,2,3,0,1:T(8,128)(2,1)} %copy.58), calls=%async_computation.2 | async-start | bytes 2097152 | tf_op jit(solution)/shard_map/all_to_all | solution.py:94
  361.7 184.4 %copy-start.10 = (bf16[1,512,128]{2,1,0:T(8,128)(2,1)S(1)}, bf16[1,512,128]{2,1,0:T(8,128)(2,1)}, u32[]{:S(2)}) copy-start(bf16[1,512,128]{2,1,0:T(8,128)(2,1)} %param.29) | copy-start | bytes 393220
where the time goes:
time: 549 us
  blocking collectives  376 us (68%)
  waiting for transfers between devices  108 us (20%)
  starting transfers between devices  28.7 us (5%)
  local copies, waits for them, and re-layouts  17.4 us (3%)
  matrix products  11.5 us (2%)
  other arithmetic  6.54 us (1%)
    all_to_all x1, blocking collectives, body(): lax.all_to_all(active, 'mp', split_axis=1, concat_axis=0, tiled=True)  184 us
    psum x1, blocking collectives, body(): sumsq_mix = lax.psum(jnp.sum(x_float * x_float, axis=2), 'mp')  73.5 us
    psum x1, blocking collectives, body(): sumsq_mlp = lax.psum(jnp.sum(resid_float * resid_float, axis=(2, 3)), 'mp')  59.3 us
    all_to_all x1, blocking collectives, body(): lax.all_to_all(closing_segment, 'ctx', split_axis=1, concat_axis=2, tiled...  59.2 us
    all_to_all x1, waiting for transfers between devices, body(): lax.all_to_all(spread, 'mp', split_axis=1, concat_axis=0, tiled=True)  58.1 us
    all_to_all x1, waiting for transfers between devices, body(): lax.all_to_all(opening_segment, 'ctx', split_axis=2, concat_axis=1, tiled...  49.1 us
    all_to_all x1, starting transfers between devices, body(): lax.all_to_all(opening_segment, 'ctx', split_axis=2, concat_axis=1, tiled...  14.6 us
  transfers between devices with their start and end apart: 3, of which 3 were waited for; matrix products, arithmetic and copies ran while one was open for 0% of the time, Pallas kernels for 0%

commit v1 on v0

v1 whole, which is shorter than its diff:
```python
import functools

import jax
import jax.numpy as jnp
from jax import lax
from jax.experimental import pallas as pl
from jax.experimental.pallas import tpu as pltpu
from jax.sharding import PartitionSpec as P

D = 1024
EPS = 1e-05
BF = jnp.bfloat16
F32 = jnp.float32
MESH = pl.DeviceIdType.MESH

SEQS = 4
TOK = 1024
CH = 128
NC = 64
NM = 8
TS = TOK // NM
STAT_ROWS = 40


def dot(a, b):
    return jnp.dot(a, b, preferred_element_type=F32)


def dot_nt(a, b):
    return lax.dot_general(a, b, (((1,), (1,)), ((), ())), preferred_element_type=F32)


def mul(v, n):
    return pl.multiple_of(v, n)


def kernel(
    x_ref,
    rim_ref,
    stat_ref,
    gain_ref,
    projin_ref,
    taps_ref,
    fi_ref,
    tw_ref,
    fo_ref,
    kern_ref,
    io_ref,
    bt_ref,
    iit_ref,
    projout_ref,
    up_ref,
    down_ref,
    out_ref,
    w1,
    w2,
    w3,
    w4,
    pw,
    upw,
    dx,
    st,
    scr,
    gain2,
    rimp,
    pj,
    src,
    q_s,
    s1,
    r1,
    sec,
    s2,
    r2,
    gt,
    g_s,
    x_s,
    h_s,
    ob,
    os_,
    st_send,
    st_recv,
    x_send,
    x_recv,
    wa_send,
    wa_recv,
    wb_send,
    wb_recv,
    c1_send,
    c1_recv,
    c2_send,
    c2_recv,
    g_send,
    g_recv,
    o_send,
    o_recv,
):
    me = lax.axis_index("ctx")
    m = lax.axis_index("mp")
    shard = (me // 16) * 2 + me % 2
    z_lo = (me // 2) % 8
    x_pos = m // 2
    z_hi = m % 2
    mate = x_pos * 2 + (1 - z_hi)

    def plane_peer(t):
        x_to = (x_pos + t // 8) % 4
        s_to = (shard + t % 8) % 8
        return (s_to // 2) * 16 + z_lo * 2 + s_to % 2, x_to * 2 + z_hi

    def remote(src_view, dst_view, send, recv, to):
        return pltpu.make_async_remote_copy(
            src_ref=src_view,
            dst_ref=dst_view,
            send_sem=send,
            recv_sem=recv,
            device_id=to,
            device_id_type=MESH,
        )

    def up_piece(b, s):
        return upw.at[b, pl.ds(mul(s * 16, 16), 16), :]

    def down_piece(b, s):
        return dx.at[
            b // 2,
            pl.ds(mul(s * 128 + (b % 2) * 64, 64), 64),
            pl.ds(mul((b % 2) * 128, 128), 128),
        ]

    def out_piece(b, s):
        return pw.at[pl.ds(mul(s * 128 + b * 16, 16), 16), pl.ds(mul(b * 128, 128), 128)]

    def clear_pw(i, c):
        pw[pl.ds(mul(i * 128, 128), 128), :] = jnp.zeros((128, 1024), BF)
        return c

    lax.fori_loop(0, 8, clear_pw, 0)

    def clear_dx(i, c):
        dx[i] = jnp.zeros((1024, 256), BF)
        return c

    lax.fori_loop(0, 4, clear_dx, 0)
    up_piece(m, shard)[...] = up_ref[pl.ds(mul(shard * 16, 16), 16), :]
    down_piece(m, shard)[...] = down_ref[pl.ds(mul(shard * 64, 64), 64), :]
    out_piece(m, shard)[...] = projout_ref[pl.ds(mul(shard * 16, 16), 16), :]
    st[m] = stat_ref[...]

    barrier = pltpu.get_barrier_semaphore()

    def greet_mp(t, c):
        pl.semaphore_signal(barrier, inc=1, device_id=(me, (m + t) % NM), device_id_type=MESH)
        return c

    lax.fori_loop(1, NM, greet_mp, 0)

    def greet_ctx(t, c):
        pl.semaphore_signal(barrier, inc=1, device_id=((me + t) % NC, m), device_id_type=MESH)
        return c

    lax.fori_loop(1, NC, greet_ctx, 0)

    def greet_plane(t, c):
        x_to = (x_pos + 1 + t // 7) % 4
        s_to = (shard + 1 + t % 7) % 8
        to = ((s_to // 2) * 16 + z_lo * 2 + s_to % 2, x_to * 2 + z_hi)
        pl.semaphore_signal(barrier, inc=1, device_id=to, device_id_type=MESH)
        return c

    lax.fori_loop(0, 21, greet_plane, 0)
    pl.semaphore_wait(barrier, (NM - 1) + (NC - 1) + 21)

    def send_stat(t, c):
        remote(st.at[m], st.at[m], st_send, st_recv, (me, (m + t) % NM)).start()
        return c

    lax.fori_loop(1, NM, send_stat, 0)
    for n, piece in enumerate((up_piece, down_piece, out_piece)):
        here = piece(m, shard)
        remote(here, here, wa_send.at[n], wa_recv.at[n], (me, mate)).start()

    def stream_copy(t):
        to = (m + t) % NM
        return remote(
            x_ref.at[:, pl.ds(mul(to * TS, TS), TS), :],
            x_s.at[:, :, pl.ds(mul(m * CH, CH), CH)],
            x_send,
            x_recv,
            (me, to),
        )

    def send_stream(t, c):
        stream_copy(t).start()
        return c

    lax.fori_loop(1, NM, send_stream, 0)
    x_s[:, :, pl.ds(mul(m * CH, CH), CH)] = x_ref[:, pl.ds(mul(m * TS, TS), TS), :]

    def build(b, c):
        rows = pl.ds(mul(b * 256, 256), 256)
        ri = b * 256 + lax.broadcasted_iota(jnp.int32, (256, 256), 0)
        ci = lax.broadcasted_iota(jnp.int32, (256, 256), 1)
        one = jnp.where(ci == (ri >> 4) * 4 + (ri & 3), 1.0, 0.0).astype(BF)
        part = dot_nt(one, fi_ref[...])
        for a in range(4):
            w1[rows, a * 256 : (a + 1) * 256] = jnp.where(((ri >> 2) & 3) == a, part, 0.0).astype(BF)
        quarter = jnp.where(ci == (ri >> 2), 1.0, 0.0).astype(BF)
        rq = lax.broadcasted_iota(jnp.int32, (256, 1024), 0)
        cq = lax.broadcasted_iota(jnp.int32, (256, 1024), 1)
        widen = jnp.where(rq == (cq >> 2), 1.0, 0.0).astype(BF)
        keep = (rq & 3) == (cq & 3)
        for factor, w in ((fo_ref, w2), (io_ref, w3)):
            part = dot_nt(quarter, factor[...]).astype(BF)
            w[rows, :] = jnp.where(keep, dot(part, widen), 0.0).astype(BF)
        pick = jnp.where(rq == (cq >> 4) * 4 + (cq & 3), 1.0, 0.0).astype(BF)
        w4[rows, :] = jnp.where(((cq >> 2) & 3) == b, dot(iit_ref[...], pick), 0.0).astype(BF)
        return c

    lax.fori_loop(0, 4, build, 0)

    remote(st.at[pl.ds(0, 7)], st.at[pl.ds(0, 7)], st_send, st_recv, (me, mate)).wait_recv()
    total = st[0]
    for b in range(1, NM):
        total = total + st[b]
    scr[...] = lax.rsqrt(total / D + EPS)
    for b in range(NM):
        gain2[:, b * CH : (b + 1) * CH] = st[b, 33:34, :]
    gain = gain_ref[...]

    def column(row):
        line = scr[pl.ds(row, 1), :]
        return jnp.transpose(jnp.broadcast_to(line, (128, 128)))

    rim_scale = column(32)[:32]
    rim_norm = (rim_ref[...].astype(F32) * rim_scale * gain).astype(BF)
    rimp[...] = dot(rim_norm, projin_ref[...]).astype(BF).astype(F32)

    def ctx_copy(t, base, out_buf, in_buf, send, recv):
        to = (me + t) % NC
        return remote(
            out_buf.at[pl.ds(mul(base + to * 16, 16), 16), :],
            in_buf.at[pl.ds(mul(base + me * 16, 16), 16), :],
            send,
            recv,
            (to, m),
        )

    def whole_ctx(base, buf, send, recv):
        view = buf.at[pl.ds(mul(base, 16), 1008), :]
        return remote(view, view, send, recv, (me, mate))

    def forward(s, c):
        base = s * TOK

        def project(b, c2):
            rows = x_ref[s, pl.ds(mul(b * 128, 128), 128), :].astype(F32)
            normed = (rows * column(s * 8 + b) * gain).astype(BF)
            pj[pl.ds(mul(8 + b * 128, 8), 128), :] = (
                dot(normed, projin_ref[...]).astype(BF).astype(F32)
            )
            return c2

        pj[0:8, :] = rimp[pl.ds(mul(s * 8, 8), 8), :]
        lax.fori_loop(0, 8, project, 0)
        for b in range(8):
            lo = b * 128
            mixed = (
                taps_ref[0:1, :] * pj[8 + lo : 136 + lo, :]
                + taps_ref[1:2, :] * pj[7 + lo : 135 + lo, :]
                + taps_ref[2:3, :] * pj[6 + lo : 134 + lo, :]
            )
            q_s[pl.ds(mul(base + lo, 128), 128), :] = mixed[:, :CH].astype(BF)
            src[lo : lo + 128, :] = (mixed[:, CH : 2 * CH] * mixed[:, 2 * CH :]).astype(BF)

        def inner(b, c2):
            rows = pl.ds(mul(b * 256, 256), 256)
            first = dot(w1[rows, :], src[...]) * tw_ref[rows, :]
            s1[pl.ds(mul(base + b * 256, 256), 256), :] = first.astype(BF)
            return c2

        lax.fori_loop(0, 4, inner, 0)

        def send(t, c2):
            ctx_copy(t, base, s1, r1, c1_send.at[s], c1_recv.at[s]).start()
            return c2

        lax.fori_loop(1, NC, send, 0)
        own = pl.ds(mul(base + me * 16, 16), 16)
        r1[own, :] = s1[own, :]
        return c

    lax.fori_loop(0, SEQS, forward, 0)

    for n, piece in enumerate((up_piece, down_piece, out_piece)):
        there = piece(mate, shard)
        remote(there, there, wa_send.at[n], wa_recv.at[n], (me, mate)).wait_recv()

    def spread_weights(t, c):
        to = plane_peer(t)
        for n, piece in enumerate((up_piece, down_piece, out_piece)):
            for b in (m, mate):
                here = piece(b, shard)
                remote(here, here, wb_send.at[n], wb_recv.at[n], to).start()
        return c

    lax.fori_loop(1, 32, spread_weights, 0)

    def middle(s, c):
        base = s * TOK
        whole_ctx(base, r1, c1_send.at[s], c1_recv.at[s]).wait_recv()

        def outer(b, c2):
            rows = pl.ds(mul(b * 256, 256), 256)
            got = r1[pl.ds(mul(base, 1024), 1024), :]
            sec[rows, :] = (dot(w2[rows, :], got) * kern_ref[rows, :].astype(F32)).astype(BF)
            return c2

        lax.fori_loop(0, 4, outer, 0)

        def back(b, c2):
            rows = pl.ds(mul(b * 256, 256), 256)
            third = dot(w3[rows, :], sec[...]) * bt_ref[rows, :]
            s2[pl.ds(mul(base + b * 256, 256), 256), :] = third.astype(BF)
            return c2

        lax.fori_loop(0, 4, back, 0)

        def send(t, c2):
            ctx_copy(t, base, s2, r2, c2_send.at[s], c2_recv.at[s]).start()
            return c2

        lax.fori_loop(1, NC, send, 0)
        own = pl.ds(mul(base + me * 16, 16), 16)
        r2[own, :] = s2[own, :]
        return c

    lax.fori_loop(0, SEQS, middle, 0)

    def gate(s, c):
        base = s * TOK
        whole_ctx(base, r2, c2_send.at[s], c2_recv.at[s]).wait_recv()

        def last(b, c2):
            rows = pl.ds(mul(b * 256, 256), 256)
            here = pl.ds(mul(base + b * 256, 256), 256)
            conv = dot(w4[rows, :], r2[pl.ds(mul(base, 1024), 1024), :])
            gt[here, :] = (q_s[here, :].astype(F32) * conv).astype(BF)
            return c2

        lax.fori_loop(0, 4, last, 0)

        def send(t, c2):
            to = (m + t) % NM
            remote(
                gt.at[pl.ds(mul(base + to * TS, TS), TS), :],
                g_s.at[s, :, pl.ds(mul(m * CH, CH), CH)],
                g_send.at[s],
                g_recv.at[s],
                (me, to),
            ).start()
            return c2

        lax.fori_loop(1, NM, send, 0)
        g_s[s, :, pl.ds(mul(m * CH, CH), CH)] = gt[pl.ds(mul(base + m * TS, TS), TS), :]
        return c

    lax.fori_loop(0, SEQS, gate, 0)

    up_all = r1.at[pl.ds(0, 62 * 64), :]
    out_all = r1.at[pl.ds(0, 62 * 16), :]
    for n, view in enumerate((up_all, up_all, out_all)):
        remote(view, view, wb_send.at[n], wb_recv.at[n], (me, mate)).wait_recv()
    x_all = x_s.at[:, :, pl.ds(0, 7 * CH)]
    remote(x_all, x_all, x_send, x_recv, (me, mate)).wait_recv()

    def finish(s, c):
        g_all = g_s.at[s, :, pl.ds(0, 7 * CH)]
        remote(g_all, g_all, g_send.at[s], g_recv.at[s], (me, mate)).wait_recv()
        resid = (x_s[s].astype(F32) + dot(g_s[s], pw[...])).astype(BF).astype(F32)
        sumsq = jnp.sum(resid * resid, axis=1, keepdims=True)
        normed = (resid * lax.rsqrt(sumsq / D + EPS) * gain2[...]).astype(BF)
        for i in range(NM):
            act = jax.nn.gelu(dot(normed[:, i * CH : (i + 1) * CH], upw[i])).astype(BF)
            for jj in range(4):
                h_s[jj, :, i * 128 : (i + 1) * 128] = act[:, jj * 128 : (jj + 1) * 128]
        for jj in range(4):
            low = dot(h_s[jj], dx[jj]) + resid[:, jj * 256 : (jj + 1) * 256]
            ob[s, 2 * jj] = low[:, :CH].astype(BF)
            ob[s, 2 * jj + 1] = low[:, CH:].astype(BF)

        rows = pl.ds(mul(s * TOK + m * TS, TS), TS)

        def send(t, c2):
            to = (m + t) % NM
            remote(ob.at[s, to], os_.at[rows, :], o_send, o_recv, (me, to)).start()
            return c2

        lax.fori_loop(1, NM, send, 0)
        os_[rows, :] = ob[s, m]
        return c

    lax.fori_loop(0, SEQS, finish, 0)

    o_all = os_.at[pl.ds(0, 28 * TS), :]
    remote(o_all, o_all, o_send, o_recv, (me, mate)).wait()
    remote(st.at[pl.ds(0, 7)], st.at[pl.ds(0, 7)], st_send, st_recv, (me, mate)).wait_send()
    for n, piece in enumerate((up_piece, down_piece, out_piece)):
        here = piece(m, shard)
        remote(here, here, wa_send.at[n], wa_recv.at[n], (me, mate)).wait_send()
    for n, view in enumerate((up_all, up_all, out_all)):
        remote(view, view, wb_send.at[n], wb_recv.at[n], (me, mate)).wait_send()
    remote(x_all, x_all, x_send, x_recv, (me, mate)).wait_send()

    def drain(s, c):
        base = s * TOK
        whole_ctx(base, s1, c1_send.at[s], c1_recv.at[s]).wait_send()
        whole_ctx(base, s2, c2_send.at[s], c2_recv.at[s]).wait_send()
        g_all = g_s.at[s, :, pl.ds(0, 7 * CH)]
        remote(g_all, g_all, g_send.at[s], g_recv.at[s], (me, mate)).wait_send()
        return c

    lax.fori_loop(0, SEQS, drain, 0)
    out_ref[...] = os_[...]


def body(
    stream,
    gain_mix,
    proj_in,
    short_taps,
    fwd_inner,
    twid_inner,
    fwd_outer,
    kernel_grid,
    inv_outer,
    backward_twiddle,
    inv_inner,
    proj_out,
    gain_mlp,
    up_blocks,
    down_blocks,
):
    pairs = [(i, i + 1) for i in range(NC - 1)]
    rim = lax.ppermute(stream[:, TOK - 8 :, :], "ctx", pairs)
    x_float = stream.astype(F32)
    rim_float = rim.astype(F32)
    sums = jnp.sum(x_float * x_float, axis=2).reshape(32, 128)
    rim_sums = jnp.sum(rim_float * rim_float, axis=2).reshape(1, 32)
    stats = jnp.concatenate(
        [
            sums,
            jnp.pad(rim_sums, ((0, 0), (0, 96))),
            gain_mlp.astype(F32).reshape(1, CH),
            jnp.zeros((STAT_ROWS - 34, 128), F32),
        ],
        axis=0,
    )
    tw = twid_inner.reshape(4, NC, 4).transpose(1, 0, 2).reshape(TOK, 1)
    bt = backward_twiddle.reshape(TOK, 1)
    operands = (
        stream,
        rim.reshape(32, CH),
        stats,
        gain_mix.astype(F32).reshape(1, CH),
        proj_in[0],
        short_taps[:, 0, :],
        fwd_inner,
        tw,
        fwd_outer,
        kernel_grid.reshape(TOK, CH),
        inv_outer,
        bt,
        inv_inner.T,
        proj_out[0],
        up_blocks[0],
        down_blocks[0],
    )
    vmem = pl.BlockSpec(memory_space=pltpu.VMEM)
    dma = pltpu.SemaphoreType.DMA
    flat = pltpu.VMEM((SEQS * TOK, CH), BF)
    square = pltpu.VMEM((1024, 1024), BF)
    out = pl.pallas_call(
        kernel,
        out_shape=jax.ShapeDtypeStruct((SEQS * TOK, CH), BF),
        in_specs=[vmem] * len(operands),
        out_specs=vmem,
        scratch_shapes=[
            square,
            square,
            square,
            square,
            square,
            pltpu.VMEM((NM, CH, 512), BF),
            pltpu.VMEM((4, 1024, 256), BF),
            pltpu.VMEM((NM, STAT_ROWS, 128), F32),
            pltpu.VMEM((STAT_ROWS, 128), F32),
            pltpu.VMEM((1, 1024), F32),
            pltpu.VMEM((32, 3 * CH), F32),
            pltpu.VMEM((8 + TOK, 3 * CH), F32),
            pltpu.VMEM((TOK, CH), BF),
            flat,
            flat,
            flat,
            pltpu.VMEM((TOK, CH), BF),
            flat,
            flat,
            flat,
            pltpu.VMEM((SEQS, TS, 1024), BF),
            pltpu.VMEM((SEQS, TS, 1024), BF),
            pltpu.VMEM((4, TS, 1024), BF),
            pltpu.VMEM((SEQS, NM, TS, CH), BF),
            flat,
            dma,
            dma,
            dma,
            dma,
            dma((3,)),
            dma((3,)),
            dma((3,)),
            dma((3,)),
            dma((SEQS,)),
            dma((SEQS,)),
            dma((SEQS,)),
            dma((SEQS,)),
            dma((SEQS,)),
            dma((SEQS,)),
            dma,
            dma,
        ],
        compiler_params=pltpu.CompilerParams(
            collective_id=0, has_side_effects=True, vmem_limit_bytes=60 * 1024 * 1024
        ),
        name="monarch_block",
    )(*operands)
    return out.reshape(SEQS, TOK, CH)


def solution(mesh):
    placed = (
        P(None, "ctx", "mp"),
        P("mp"),
        P("mp", None, None),
        P(None, "mp", None),
        P(),
        P("ctx", None),
        P(),
        P(None, "ctx", "mp"),
        P(),
        P(None, "ctx"),
        P(),
        P("mp", None, None),
        P("mp"),
        P("mp", None, None),
        P("mp", None, None),
    )
    return jax.shard_map(
        body, mesh=mesh, in_specs=placed, out_specs=P(None, "ctx", "mp"), check_vma=False
    )
```

time: 549 us -> 323 us (0.59)
  the two profiles are of different devices: /device:TPU:41 before, /device:TPU:65 now
where the time goes in v1:
time: 323 us
  Pallas kernels  308 us (95%)
  local copies, waits for them, and re-layouts  6.9 us (2%)
  other arithmetic  4.48 us (1%)
  starting transfers between devices  4.09 us (1%)
    pallas_call x1, Pallas kernels, body(): pl.pallas_call(kernel, out_shape=jax.ShapeDtypeStruct((SEQS * TOK, CH), B...  308 us
  transfers between devices with their start and end apart: 1, of which 0 were waited for; matrix products, arithmetic and copies ran while one was open for 2% of the time, Pallas kernels for 0%

profile of v1, /device:TPU:65, one launch (start us, length us, event | category | flops | bytes accessed | tf_op | source)
XLA Modules:
  0.0 323.2 jit_solution(1304879262071549404)
XLA Ops:
  0.0 0.0 copy-start.2
  0.0 0.0 copy-start.3
  0.0 0.0 copy-start.4
  0.0 0.0 copy-start
  0.0 0.8 slice.3
  0.8 4.1 %collective-permute-start = (bf16[4,8,128]{2,1,0:T(8,128)(2,1)S(1)}, bf16[4,8,128]{2,1,0:T(8,128)(2,1)S(1)}, u32[]{:S(2)}, u32[]{:S(2)}) collective-permute-start(bf16[4,8,128]{2,1,0:T(8,128)(2,1)S(1)} %slice.3), channel_id=1, source_target_pairs={{0,8},{8,16},{16,24},{24,32},{32,40},{40,48},{48,56},{56,64},{64,7... | collective-permute-start | bytes 24584 | tf_op jit(solution)/shard_map/ppermute | solution.py:444
  4.9 1.2 bitcast_convert_fusion.gain_ref
  6.1 0.7 bitcast_convert_fusion.1
  6.7 1.8 multiply_reduce_fusion
  8.6 0.0 copy-done.2
  8.6 0.6 copy.26
  9.2 0.0 copy-done.3
  9.2 0.1 reshape.42
  9.4 0.1 copy.19
  9.5 0.0 copy-done.4
  9.5 0.1 copy.20
  9.6 0.0 copy-done
  9.6 0.8 copy.21
  10.4 1.0 reshape.52.bt_ref
  11.4 1.0 reshape.51.tw_ref
  12.4 0.1 pad.8.clone
  12.4 0.0 collective-permute-done
  12.4 0.0 copy-start.1
  12.4 0.1 multiply_reduce_fusion.1
  12.5 0.1 reshape.37
  12.6 0.7 fusion.1.stat_ref
  13.3 0.0 copy-done.1
  13.3 307.6 %monarch_block.1 = bf16[4096,128]{1,0:T(8,128)(2,1)} custom-call(bf16[4,1024,128]{2,1,0:T(8,128)(2,1)} %x_ref.1, bf16[32,128]{1,0:T(8,128)(2,1)} %bitcast.26, f32[40,128]{1,0:T(8,128)} %fusion.1.stat_ref, f32[1,128]{1,0:T(1,128)} %bitcast_convert_fusion.gain_ref, bf16[128,384]{1,0:T(8,128)(2,1)} %bitcast.24, f32[3,384]{1,0:T(4,128)} %bitcast.27, ...), custom_call_target="tpu_custom_call" | custom-call | tf_op jit(solution)/shard_map/monarch_block/pallas_call | solution.py:482
  320.9 2.3 copy.28
  (2 shorter events, 0.0 us)
Async XLA Ops:
  0.0 8.6 %copy-start.2 = (f32[3,1,384]{2,1,0:T(1,128)S(1)}, f32[3,1,384]{2,1,0:T(1,128)}, u32[]{:S(2)}) copy-start(f32[3,1,384]{2,1,0:T(1,128)} %param.18) | copy-start | bytes 13828
  0.0 9.2 %copy-start.3 = (f32[4,256]{1,0:T(4,128)S(1)}, f32[4,256]{1,0:T(4,128)}, u32[]{:S(2)}) copy-start(f32[4,256]{1,0:T(4,128)} %param.20) | copy-start | bytes 12292
  0.0 9.5 %copy-start.4 = (f32[256,4]{0,1:T(4,128)S(1)}, f32[256,4]{0,1:T(4,128)}, u32[]{:S(2)}) copy-start(f32[256,4]{0,1:T(4,128)} %param.24) | copy-start | bytes 12292
  0.0 9.6 %copy-start = (bf16[256,256]{1,0:T(8,128)(2,1)S(1)}, bf16[256,256]{1,0:T(8,128)(2,1)}, u32[]{:S(2)}) copy-start(bf16[256,256]{1,0:T(8,128)(2,1)} %param.25) | copy-start | bytes 393220
  0.8 11.7 %collective-permute-start = (bf16[4,8,128]{2,1,0:T(8,128)(2,1)S(1)}, bf16[4,8,128]{2,1,0:T(8,128)(2,1)S(1)}, u32[]{:S(2)}, u32[]{:S(2)}) collective-permute-start(bf16[4,8,128]{2,1,0:T(8,128)(2,1)S(1)} %slice.3), channel_id=1, source_target_pairs={{0,8},{8,16},{16,24},{24,32},{32,40},{40,48},{48,56},{56,64},{64,7... | collective-permute-start | bytes 24584 | tf_op jit(solution)/shard_map/ppermute | solution.py:444
  12.4 0.9 copy-start.1

commit v2 on v1

--- a/solution.py
+++ b/solution.py
@@ -36,8 +36,6 @@
 
 def kernel(
     x_ref,
-    rim_ref,
-    stat_ref,
     gain_ref,
     projin_ref,
     taps_ref,
@@ -47,7 +45,7 @@
     kern_ref,
     io_ref,
     bt_ref,
-    iit_ref,
+    ii_ref,
     projout_ref,
     up_ref,
     down_ref,
@@ -60,6 +58,11 @@
     upw,
     dx,
     st,
+    rt,
+    rr,
+    rimx,
+    twb,
+    btb,
     scr,
     gain2,
     rimp,
@@ -85,6 +88,12 @@
     wa_recv,
     wb_send,
     wb_recv,
+    ws_send,
+    ws_recv,
+    rt_send,
+    rt_recv,
+    rx_send,
+    rx_recv,
     c1_send,
     c1_recv,
     c2_send,
@@ -96,16 +105,21 @@
 ):
     me = lax.axis_index("ctx")
     m = lax.axis_index("mp")
-    shard = (me // 16) * 2 + me % 2
+    core = me % 2
+    y_pos = me // 16
     z_lo = (me // 2) % 8
+    shard = core * 4 + y_pos
     x_pos = m // 2
     z_hi = m % 2
     mate = x_pos * 2 + (1 - z_hi)
+    twin = me + 1 - 2 * core
+    after = (me + 1) % NC
+    before = (me + NC - 1) % NC
 
     def plane_peer(t):
-        x_to = (x_pos + t // 8) % 4
-        s_to = (shard + t % 8) % 8
-        return (s_to // 2) * 16 + z_lo * 2 + s_to % 2, x_to * 2 + z_hi
+        x_to = (x_pos + t // 4) % 4
+        y_to = (y_pos + t % 4) % 4
+        return y_to * 16 + z_lo * 2 + core, x_to * 2 + z_hi
 
     def remote(src_view, dst_view, send, recv, to):
         return pltpu.make_async_remote_copy(
@@ -141,43 +155,83 @@
         return c
 
     lax.fori_loop(0, 4, clear_dx, 0)
+    barrier = pltpu.get_barrier_semaphore()
+
+    def greet_mp(t, c):
+        pl.semaphore_signal(barrier, inc=1, device_id=(me, (m + t) % NM), device_id_type=MESH)
+        return c
+
+    lax.fori_loop(1, NM, greet_mp, 0)
+
+    def greet_ctx(t, c):
+        pl.semaphore_signal(barrier, inc=1, device_id=((me + t) % NC, m), device_id_type=MESH)
+        return c
+
+    lax.fori_loop(1, NC, greet_ctx, 0)
+
+    def greet_plane(t, c):
+        to = plane_peer(4 * (1 + t // 3) + 1 + t % 3)
+        pl.semaphore_signal(barrier, inc=1, device_id=to, device_id_type=MESH)
+        return c
+
+    lax.fori_loop(0, 9, greet_plane, 0)
+
+    def greet_rim(t, c):
+        to = (m + t) % NM
+        pl.semaphore_signal(barrier, inc=1, device_id=(after, to), device_id_type=MESH)
+        pl.semaphore_signal(barrier, inc=1, device_id=(before, to), device_id_type=MESH)
+        return c
+
+    lax.fori_loop(1, NM, greet_rim, 0)
+
     up_piece(m, shard)[...] = up_ref[pl.ds(mul(shard * 16, 16), 16), :]
     down_piece(m, shard)[...] = down_ref[pl.ds(mul(shard * 64, 64), 64), :]
     out_piece(m, shard)[...] = projout_ref[pl.ds(mul(shard * 16, 16), 16), :]
-    st[m] = stat_ref[...]
-
-    barrier = pltpu.get_barrier_semaphore()
-
-    def greet_mp(t, c):
-        pl.semaphore_signal(barrier, inc=1, device_id=(me, (m + t) % NM), device_id_type=MESH)
-        return c
-
-    lax.fori_loop(1, NM, greet_mp, 0)
-
-    def greet_ctx(t, c):
-        pl.semaphore_signal(barrier, inc=1, device_id=((me + t) % NC, m), device_id_type=MESH)
-        return c
-
-    lax.fori_loop(1, NC, greet_ctx, 0)
-
-    def greet_plane(t, c):
-        x_to = (x_pos + 1 + t // 7) % 4
-        s_to = (shard + 1 + t % 7) % 8
-        to = ((s_to // 2) * 16 + z_lo * 2 + s_to % 2, x_to * 2 + z_hi)
-        pl.semaphore_signal(barrier, inc=1, device_id=to, device_id_type=MESH)
-        return c
-
-    lax.fori_loop(0, 21, greet_plane, 0)
-    pl.semaphore_wait(barrier, (NM - 1) + (NC - 1) + 21)
+    ones = jnp.ones((8, CH), BF)
+    rt[...] = jnp.zeros((8, 128), F32)
+    st[m, 32:40, :] = jnp.broadcast_to(gain_ref[1:2, :], (8, 128))
+
+    def sums(s, c):
+        for b in range(8):
+            rows = x_ref[s, b * 128 : (b + 1) * 128, :].astype(F32)
+            square = rows * rows
+            high = square.astype(BF)
+            low = (square - high.astype(F32)).astype(BF)
+            line = (dot_nt(ones, high) + dot_nt(ones, low))[0:1]
+            st[m, pl.ds(s * 8 + b, 1), :] = line
+            if b == 7:
+                rt[pl.ds(s, 1), :] = line
+        return c
+
+    lax.fori_loop(0, SEQS, sums, 0)
+    pl.semaphore_wait(barrier, (NM - 1) + (NC - 1) + 9 + 2 * (NM - 1))
 
     def send_stat(t, c):
         remote(st.at[m], st.at[m], st_send, st_recv, (me, (m + t) % NM)).start()
         return c
 
     lax.fori_loop(1, NM, send_stat, 0)
+
+    def send_rim(t, c):
+        remote(rt, rr.at[m], rt_send, rt_recv, (after, (m + t) % NM)).start()
+        return c
+
+    lax.fori_loop(0, NM, send_rim, 0)
+    remote(x_ref.at[:, pl.ds(TOK - 16, 16), :], rimx, rx_send, rx_recv, (after, m)).start()
     for n, piece in enumerate((up_piece, down_piece, out_piece)):
         here = piece(m, shard)
         remote(here, here, wa_send.at[n], wa_recv.at[n], (me, mate)).start()
+
+    def spread(block):
+        def send(t, c):
+            for n, piece in enumerate((up_piece, down_piece, out_piece)):
+                here = piece(block, shard)
+                remote(here, here, wb_send.at[n], wb_recv.at[n], plane_peer(t)).start()
+            return c
+
+        lax.fori_loop(1, 16, send, 0)
+
+    spread(m)
 
     def stream_copy(t):
         to = (m + t) % NM
@@ -196,6 +250,10 @@
     lax.fori_loop(1, NM, send_stream, 0)
     x_s[:, :, pl.ds(mul(m * CH, CH), CH)] = x_ref[:, pl.ds(mul(m * TS, TS), TS), :]
 
+    eye_r = lax.broadcasted_iota(jnp.int32, (256, 256), 0)
+    eye_c = lax.broadcasted_iota(jnp.int32, (256, 256), 1)
+    turned = dot_nt(jnp.where(eye_r == eye_c, 1.0, 0.0).astype(BF), ii_ref[...]).astype(BF)
+
     def build(b, c):
         rows = pl.ds(mul(b * 256, 256), 256)
         ri = b * 256 + lax.broadcasted_iota(jnp.int32, (256, 256), 0)
@@ -205,6 +263,21 @@
         for a in range(4):
             w1[rows, a * 256 : (a + 1) * 256] = jnp.where(((ri >> 2) & 3) == a, part, 0.0).astype(BF)
         quarter = jnp.where(ci == (ri >> 2), 1.0, 0.0).astype(BF)
+        lane = lax.broadcasted_iota(jnp.int32, (256, 4), 1)
+        row = b * 256 + lax.broadcasted_iota(jnp.int32, (256, 4), 0)
+        for hot, factor, which, to in (
+            (one, tw_ref, (row >> 2) & 3, twb),
+            (quarter, bt_ref, row & 3, btb),
+        ):
+            part = lax.dot_general(
+                hot.astype(F32),
+                factor[...],
+                (((1,), (1,)), ((), ())),
+                precision=lax.Precision.HIGHEST,
+                preferred_element_type=F32,
+            )
+            line = jnp.sum(jnp.where(lane == which, part, 0.0), axis=1, keepdims=True)
+            to[rows, :] = jnp.broadcast_to(line, (256, 128))
         rq = lax.broadcasted_iota(jnp.int32, (256, 1024), 0)
         cq = lax.broadcasted_iota(jnp.int32, (256, 1024), 1)
         widen = jnp.where(rq == (cq >> 2), 1.0, 0.0).astype(BF)
@@ -213,7 +286,7 @@
             part = dot_nt(quarter, factor[...]).astype(BF)
             w[rows, :] = jnp.where(keep, dot(part, widen), 0.0).astype(BF)
         pick = jnp.where(rq == (cq >> 4) * 4 + (cq & 3), 1.0, 0.0).astype(BF)
-        w4[rows, :] = jnp.where(((cq >> 2) & 3) == b, dot(iit_ref[...], pick), 0.0).astype(BF)
+        w4[rows, :] = jnp.where(((cq >> 2) & 3) == b, dot(turned, pick), 0.0).astype(BF)
         return c
 
     lax.fori_loop(0, 4, build, 0)
@@ -222,18 +295,26 @@
     total = st[0]
     for b in range(1, NM):
         total = total + st[b]
-    scr[...] = lax.rsqrt(total / D + EPS)
+    scr[0:STAT_ROWS, :] = lax.rsqrt(total / D + EPS)
     for b in range(NM):
-        gain2[:, b * CH : (b + 1) * CH] = st[b, 33:34, :]
-    gain = gain_ref[...]
+        gain2[:, b * CH : (b + 1) * CH] = st[b, 32:33, :]
+    gain = gain_ref[0:1, :]
 
     def column(row):
         line = scr[pl.ds(row, 1), :]
         return jnp.transpose(jnp.broadcast_to(line, (128, 128)))
 
-    rim_scale = column(32)[:32]
-    rim_norm = (rim_ref[...].astype(F32) * rim_scale * gain).astype(BF)
-    rimp[...] = dot(rim_norm, projin_ref[...]).astype(BF).astype(F32)
+    remote(rr, rr, rt_send, rt_recv, (me, mate)).wait_recv()
+    remote(rimx, rimx, rx_send, rx_recv, (me, mate)).wait_recv()
+    total = rr[0]
+    for b in range(1, NM):
+        total = total + rr[b]
+    scr[STAT_ROWS : STAT_ROWS + 8, :] = lax.rsqrt(total / D + EPS)
+    for s in range(SEQS):
+        rows = rimx[s].astype(F32)[8:16] * column(STAT_ROWS + s)[120:128] * gain
+        edge = dot(jnp.concatenate([rows, rows], 0).astype(BF), projin_ref[...])[:8]
+        edge = edge.astype(BF).astype(F32)
+        rimp[s * 8 : s * 8 + 8, :] = jnp.where(me > 0, edge, 0.0)
 
     def ctx_copy(t, base, out_buf, in_buf, send, recv):
         to = (me + t) % NC
@@ -265,16 +346,16 @@
         for b in range(8):
             lo = b * 128
             mixed = (
-                taps_ref[0:1, :] * pj[8 + lo : 136 + lo, :]
-                + taps_ref[1:2, :] * pj[7 + lo : 135 + lo, :]
-                + taps_ref[2:3, :] * pj[6 + lo : 134 + lo, :]
+                taps_ref[0] * pj[8 + lo : 136 + lo, :]
+                + taps_ref[1] * pj[7 + lo : 135 + lo, :]
+                + taps_ref[2] * pj[6 + lo : 134 + lo, :]
             )
             q_s[pl.ds(mul(base + lo, 128), 128), :] = mixed[:, :CH].astype(BF)
             src[lo : lo + 128, :] = (mixed[:, CH : 2 * CH] * mixed[:, 2 * CH :]).astype(BF)
 
         def inner(b, c2):
             rows = pl.ds(mul(b * 256, 256), 256)
-            first = dot(w1[rows, :], src[...]) * tw_ref[rows, :]
+            first = dot(w1[rows, :], src[...]) * twb[rows, :]
             s1[pl.ds(mul(base + b * 256, 256), 256), :] = first.astype(BF)
             return c2
 
@@ -287,23 +368,32 @@
         lax.fori_loop(1, NC, send, 0)
         own = pl.ds(mul(base + me * 16, 16), 16)
         r1[own, :] = s1[own, :]
+
+        @pl.when(s == 0)
+        def _():
+            for n, piece in enumerate((up_piece, down_piece, out_piece)):
+                there = piece(mate, shard)
+                remote(there, there, wa_send.at[n], wa_recv.at[n], (me, mate)).wait_recv()
+            spread(mate)
+
         return c
 
     lax.fori_loop(0, SEQS, forward, 0)
 
-    for n, piece in enumerate((up_piece, down_piece, out_piece)):
-        there = piece(mate, shard)
-        remote(there, there, wa_send.at[n], wa_recv.at[n], (me, mate)).wait_recv()
-
-    def spread_weights(t, c):
-        to = plane_peer(t)
-        for n, piece in enumerate((up_piece, down_piece, out_piece)):
-            for b in (m, mate):
-                here = piece(b, shard)
-                remote(here, here, wb_send.at[n], wb_recv.at[n], to).start()
-        return c
-
-    lax.fori_loop(1, 32, spread_weights, 0)
+    up_all = r1.at[pl.ds(0, 30 * 64), :]
+    out_all = r1.at[pl.ds(0, 30 * 16), :]
+    for n, view in enumerate((up_all, up_all, out_all)):
+        remote(view, view, wb_send.at[n], wb_recv.at[n], (me, mate)).wait_recv()
+
+    def halves(side):
+        return (
+            upw.at[:, pl.ds(mul(side * 64, 64), 64), :],
+            dx.at[:, pl.ds(mul(side * 512, 512), 512), :],
+            pw.at[pl.ds(mul(side * 512, 512), 512), :],
+        )
+
+    for n, half in enumerate(halves(core)):
+        remote(half, half, ws_send.at[n], ws_recv.at[n], (twin, m)).start()
 
     def middle(s, c):
         base = s * TOK
@@ -319,7 +409,7 @@
 
         def back(b, c2):
             rows = pl.ds(mul(b * 256, 256), 256)
-            third = dot(w3[rows, :], sec[...]) * bt_ref[rows, :]
+            third = dot(w3[rows, :], sec[...]) * btb[rows, :]
             s2[pl.ds(mul(base + b * 256, 256), 256), :] = third.astype(BF)
             return c2
 
@@ -366,10 +456,8 @@
 
     lax.fori_loop(0, SEQS, gate, 0)
 
-    up_all = r1.at[pl.ds(0, 62 * 64), :]
-    out_all = r1.at[pl.ds(0, 62 * 16), :]
-    for n, view in enumerate((up_all, up_all, out_all)):
-        remote(view, view, wb_send.at[n], wb_recv.at[n], (me, mate)).wait_recv()
+    for n, half in enumerate(halves(1 - core)):
+        remote(half, half, ws_send.at[n], ws_recv.at[n], (twin, m)).wait_recv()
     x_all = x_s.at[:, :, pl.ds(0, 7 * CH)]
     remote(x_all, x_all, x_send, x_recv, (me, mate)).wait_recv()
 
@@ -410,6 +498,10 @@
     for n, view in enumerate((up_all, up_all, out_all)):
         remote(view, view, wb_send.at[n], wb_recv.at[n], (me, mate)).wait_send()
     remote(x_all, x_all, x_send, x_recv, (me, mate)).wait_send()
+    for n, half in enumerate(halves(core)):
+        remote(half, half, ws_send.at[n], ws_recv.at[n], (twin, m)).wait_send()
+    remote(rr, rr, rt_send, rt_recv, (me, mate)).wait_send()
+    remote(rimx, rimx, rx_send, rx_recv, (me, mate)).wait_send()
 
     def drain(s, c):
         base = s * TOK
@@ -440,37 +532,19 @@
     up_blocks,
     down_blocks,
 ):
-    pairs = [(i, i + 1) for i in range(NC - 1)]
-    rim = lax.ppermute(stream[:, TOK - 8 :, :], "ctx", pairs)
-    x_float = stream.astype(F32)
-    rim_float = rim.astype(F32)
-    sums = jnp.sum(x_float * x_float, axis=2).reshape(32, 128)
-    rim_sums = jnp.sum(rim_float * rim_float, axis=2).reshape(1, 32)
-    stats = jnp.concatenate(
-        [
-            sums,
-            jnp.pad(rim_sums, ((0, 0), (0, 96))),
-            gain_mlp.astype(F32).reshape(1, CH),
-            jnp.zeros((STAT_ROWS - 34, 128), F32),
-        ],
-        axis=0,
-    )
-    tw = twid_inner.reshape(4, NC, 4).transpose(1, 0, 2).reshape(TOK, 1)
-    bt = backward_twiddle.reshape(TOK, 1)
+    gains = jnp.stack([gain_mix, gain_mlp]).astype(F32)
     operands = (
         stream,
-        rim.reshape(32, CH),
-        stats,
-        gain_mix.astype(F32).reshape(1, CH),
+        gains,
         proj_in[0],
-        short_taps[:, 0, :],
+        short_taps,
         fwd_inner,
-        tw,
+        twid_inner,
         fwd_outer,
         kernel_grid.reshape(TOK, CH),
         inv_outer,
-        bt,
-        inv_inner.T,
+        backward_twiddle.T,
+        inv_inner,
         proj_out[0],
         up_blocks[0],
         down_blocks[0],
@@ -493,7 +567,12 @@
             pltpu.VMEM((NM, CH, 512), BF),
             pltpu.VMEM((4, 1024, 256), BF),
             pltpu.VMEM((NM, STAT_ROWS, 128), F32),
-            pltpu.VMEM((STAT_ROWS, 128), F32),
+            pltpu.VMEM((8, 128), F32),
+            pltpu.VMEM((NM, 8, 128), F32),
+            pltpu.VMEM((SEQS, 16, CH), BF),
+            pltpu.VMEM((TOK, 128), F32),
+            pltpu.VMEM((TOK, 128), F32),
+            pltpu.VMEM((STAT_ROWS + 8, 128), F32),
             pltpu.VMEM((1, 1024), F32),
             pltpu.VMEM((32, 3 * CH), F32),
             pltpu.VMEM((8 + TOK, 3 * CH), F32),
@@ -518,6 +597,12 @@
             dma((3,)),
             dma((3,)),
             dma((3,)),
+            dma((3,)),
+            dma((3,)),
+            dma,
+            dma,
+            dma,
+            dma,
             dma((SEQS,)),
             dma((SEQS,)),
             dma((SEQS,)),

time: 323 us -> 312 us (0.966)
  the two profiles are of different devices: /device:TPU:65 before, /device:TPU:176 now
where the time goes in v2:
time: 312 us
  Pallas kernels  308 us (99%)
    pallas_call x1, Pallas kernels, body(): pl.pallas_call(kernel, out_shape=jax.ShapeDtypeStruct((SEQS * TOK, CH), B...  308 us

profile of v2, /device:TPU:176, one launch (start us, length us, event | category | flops | bytes accessed | tf_op | source)
XLA Modules:
  0.0 311.6 jit_solution(9833039166414615706)
XLA Ops:
  0.0 0.0 copy-start
  0.0 0.0 copy-start.1
  0.0 0.7 copy-done
  0.7 0.0 copy-done.1
  0.7 0.6 maximum_convert_fusion.gain_ref
  1.2 308.1 %monarch_block.1 = bf16[4096,128]{1,0:T(8,128)(2,1)} custom-call(bf16[4,1024,128]{2,1,0:T(8,128)(2,1)} %x_ref.1, f32[2,128]{1,0:T(2,128)} %maximum_convert_fusion.gain_ref, bf16[128,384]{1,0:T(8,128)(2,1)} %bitcast.13, f32[3,1,384]{2,1,0:T(1,128)} %taps_ref.1, bf16[256,256]{1,0:T(8,128)(2,1)} %fi_ref.1, f32[4,256]{1,0:T(4,128)} %tw_ref.1, ...), custom_call_target="tpu_custom_call" | custom-call | tf_op jit(solution)/shard_map/monarch_block/pallas_call | solution.py:556
  309.3 2.3 copy.17
Async XLA Ops:
  0.0 0.7 copy-start
  0.0 0.7 copy-start.1

commit v3 on v2

--- a/solution.py
+++ b/solution.py
@@ -233,21 +233,22 @@
 
     spread(m)
 
-    def stream_copy(t):
-        to = (m + t) % NM
-        return remote(
-            x_ref.at[:, pl.ds(mul(to * TS, TS), TS), :],
-            x_s.at[:, :, pl.ds(mul(m * CH, CH), CH)],
-            x_send,
-            x_recv,
-            (me, to),
-        )
-
-    def send_stream(t, c):
-        stream_copy(t).start()
-        return c
-
-    lax.fori_loop(1, NM, send_stream, 0)
+    def send_stream(s):
+        def send(t, c):
+            to = (m + t) % NM
+            remote(
+                x_ref.at[s, pl.ds(mul(to * TS, TS), TS), :],
+                x_s.at[s, :, pl.ds(mul(m * CH, CH), CH)],
+                x_send.at[s],
+                x_recv.at[s],
+                (me, to),
+            ).start()
+            return c
+
+        lax.fori_loop(1, NM, send, 0)
+
+    for s in range(SEQS):
+        send_stream(s)
     x_s[:, :, pl.ds(mul(m * CH, CH), CH)] = x_ref[:, pl.ds(mul(m * TS, TS), TS), :]
 
     eye_r = lax.broadcasted_iota(jnp.int32, (256, 256), 0)
@@ -330,6 +331,13 @@
         view = buf.at[pl.ds(mul(base, 16), 1008), :]
         return remote(view, view, send, recv, (me, mate))
 
+    def send_first(s):
+        def send(t, c):
+            ctx_copy(t, s * TOK, s1, r1, c1_send.at[s], c1_recv.at[s]).start()
+            return c
+
+        lax.fori_loop(1, NC, send, 0)
+
     def forward(s, c):
         base = s * TOK
 
@@ -361,11 +369,8 @@
 
         lax.fori_loop(0, 4, inner, 0)
 
-        def send(t, c2):
-            ctx_copy(t, base, s1, r1, c1_send.at[s], c1_recv.at[s]).start()
-            return c2
-
-        lax.fori_loop(1, NC, send, 0)
+        send_first(s)
+
         own = pl.ds(mul(base + me * 16, 16), 16)
         r1[own, :] = s1[own, :]
 
@@ -399,6 +404,7 @@
         base = s * TOK
         whole_ctx(base, r1, c1_send.at[s], c1_recv.at[s]).wait_recv()
 
+
         def outer(b, c2):
             rows = pl.ds(mul(b * 256, 256), 256)
             got = r1[pl.ds(mul(base, 1024), 1024), :]
@@ -426,9 +432,14 @@
 
     lax.fori_loop(0, SEQS, middle, 0)
 
+    def gate_in(s, c):
+        whole_ctx(s * TOK, r2, c2_send.at[s], c2_recv.at[s]).wait_recv()
+        return c
+
+    lax.fori_loop(0, SEQS, gate_in, 0)
+
     def gate(s, c):
         base = s * TOK
-        whole_ctx(base, r2, c2_send.at[s], c2_recv.at[s]).wait_recv()
 
         def last(b, c2):
             rows = pl.ds(mul(b * 256, 256), 256)
@@ -458,12 +469,11 @@
 
     for n, half in enumerate(halves(1 - core)):
         remote(half, half, ws_send.at[n], ws_recv.at[n], (twin, m)).wait_recv()
-    x_all = x_s.at[:, :, pl.ds(0, 7 * CH)]
-    remote(x_all, x_all, x_send, x_recv, (me, mate)).wait_recv()
 
     def finish(s, c):
         g_all = g_s.at[s, :, pl.ds(0, 7 * CH)]
         remote(g_all, g_all, g_send.at[s], g_recv.at[s], (me, mate)).wait_recv()
+        remote(g_all, g_all, x_send.at[s], x_recv.at[s], (me, mate)).wait_recv()
         resid = (x_s[s].astype(F32) + dot(g_s[s], pw[...])).astype(BF).astype(F32)
         sumsq = jnp.sum(resid * resid, axis=1, keepdims=True)
         normed = (resid * lax.rsqrt(sumsq / D + EPS) * gain2[...]).astype(BF)
@@ -497,7 +507,6 @@
         remote(here, here, wa_send.at[n], wa_recv.at[n], (me, mate)).wait_send()
     for n, view in enumerate((up_all, up_all, out_all)):
         remote(view, view, wb_send.at[n], wb_recv.at[n], (me, mate)).wait_send()
-    remote(x_all, x_all, x_send, x_recv, (me, mate)).wait_send()
     for n, half in enumerate(halves(core)):
         remote(half, half, ws_send.at[n], ws_recv.at[n], (twin, m)).wait_send()
     remote(rr, rr, rt_send, rt_recv, (me, mate)).wait_send()
@@ -509,6 +518,7 @@
         whole_ctx(base, s2, c2_send.at[s], c2_recv.at[s]).wait_send()
         g_all = g_s.at[s, :, pl.ds(0, 7 * CH)]
         remote(g_all, g_all, g_send.at[s], g_recv.at[s], (me, mate)).wait_send()
+        remote(g_all, g_all, x_send.at[s], x_recv.at[s], (me, mate)).wait_send()
         return c
 
     lax.fori_loop(0, SEQS, drain, 0)
@@ -591,8 +601,8 @@
             flat,
             dma,
             dma,
-            dma,
-            dma,
+            dma((SEQS,)),
+            dma((SEQS,)),
             dma((3,)),
             dma((3,)),
             dma((3,)),

time: 312 us -> 274 us (0.88)
  the two profiles are of different devices: /device:TPU:176 before, /device:TPU:32 now
where the time goes in v3:
time: 274 us
  Pallas kernels  270 us (99%)
  local copies, waits for them, and re-layouts  2.93 us (1%)
    pallas_call x1, Pallas kernels, body(): pl.pallas_call(kernel, out_shape=jax.ShapeDtypeStruct((SEQS * TOK, CH), B...  270 us

profile of v3, /device:TPU:32, one launch (start us, length us, event | category | flops | bytes accessed | tf_op | source)
XLA Modules:
  0.0 273.5 jit_solution(587231378133464242)
XLA Ops:
  0.0 0.0 copy-start
  0.0 0.0 copy-start.1
  0.0 0.7 copy-done
  0.7 0.0 copy-done.1
  0.7 0.6 maximum_convert_fusion.gain_ref
  1.2 270.0 %monarch_block.1 = bf16[4096,128]{1,0:T(8,128)(2,1)} custom-call(bf16[4,1024,128]{2,1,0:T(8,128)(2,1)} %x_ref.1, f32[2,128]{1,0:T(2,128)} %maximum_convert_fusion.gain_ref, bf16[128,384]{1,0:T(8,128)(2,1)} %bitcast.13, f32[3,1,384]{2,1,0:T(1,128)} %taps_ref.1, bf16[256,256]{1,0:T(8,128)(2,1)} %fi_ref.1, f32[4,256]{1,0:T(4,128)} %tw_ref.1, ...), custom_call_target="tpu_custom_call" | custom-call | tf_op jit(solution)/shard_map/monarch_block/pallas_call | solution.py:566
  271.3 2.3 copy.17
Async XLA Ops:
  0.0 0.7 copy-start
  0.0 0.7 copy-start.1

commit v4 on v3

--- a/solution.py
+++ b/solution.py
@@ -432,14 +432,9 @@
 
     lax.fori_loop(0, SEQS, middle, 0)
 
-    def gate_in(s, c):
-        whole_ctx(s * TOK, r2, c2_send.at[s], c2_recv.at[s]).wait_recv()
-        return c
-
-    lax.fori_loop(0, SEQS, gate_in, 0)
-
     def gate(s, c):
         base = s * TOK
+        whole_ctx(base, r2, c2_send.at[s], c2_recv.at[s]).wait_recv()
 
         def last(b, c2):
             rows = pl.ds(mul(b * 256, 256), 256)
@@ -449,6 +444,12 @@
             return c2
 
         lax.fori_loop(0, 4, last, 0)
+        return c
+
+    lax.fori_loop(0, SEQS, gate, 0)
+
+    def gated_out(s, c):
+        base = s * TOK
 
         def send(t, c2):
             to = (m + t) % NM
@@ -465,7 +466,7 @@
         g_s[s, :, pl.ds(mul(m * CH, CH), CH)] = gt[pl.ds(mul(base + m * TS, TS), TS), :]
         return c
 
-    lax.fori_loop(0, SEQS, gate, 0)
+    lax.fori_loop(0, SEQS, gated_out, 0)
 
     for n, half in enumerate(halves(1 - core)):
         remote(half, half, ws_send.at[n], ws_recv.at[n], (twin, m)).wait_recv()

time: 274 us -> 274 us (level)
  no operation moved by 1% of the time
where the time goes in v4:
time: 274 us
  Pallas kernels  270 us (99%)
  local copies, waits for them, and re-layouts  2.93 us (1%)
    pallas_call x1, Pallas kernels, body(): pl.pallas_call(kernel, out_shape=jax.ShapeDtypeStruct((SEQS * TOK, CH), B...  270 us

profile of v4, /device:TPU:32, one launch (start us, length us, event | category | flops | bytes accessed | tf_op | source)
XLA Modules:
  0.0 273.5 jit_solution(8027907645971068178)
XLA Ops:
  0.0 0.0 copy-start
  0.0 0.0 copy-start.1
  0.0 0.7 copy-done
  0.7 0.0 copy-done.1
  0.7 0.6 maximum_convert_fusion.gain_ref
  1.2 270.0 %monarch_block.1 = bf16[4096,128]{1,0:T(8,128)(2,1)} custom-call(bf16[4,1024,128]{2,1,0:T(8,128)(2,1)} %x_ref.1, f32[2,128]{1,0:T(2,128)} %maximum_convert_fusion.gain_ref, bf16[128,384]{1,0:T(8,128)(2,1)} %bitcast.13, f32[3,1,384]{2,1,0:T(1,128)} %taps_ref.1, bf16[256,256]{1,0:T(8,128)(2,1)} %fi_ref.1, f32[4,256]{1,0:T(4,128)} %tw_ref.1, ...), custom_call_target="tpu_custom_call" | custom-call | tf_op jit(solution)/shard_map/monarch_block/pallas_call | solution.py:567
  271.3 2.3 copy.17
Async XLA Ops:
  0.0 0.7 copy-start
  0.0 0.7 copy-start.1
